TPU v7x, 512 devices: a whole 4x8x8 slice. The times are simulated.
512 devices in a mesh: dp: 2 (over core), ctx: 64 (over z, y), head: 4 (over x).
Axes of the slice: x: 4, y: 8, z: 8, core: 2. Of those that a mesh axis runs over, the one named last changes fastest.
Arguments:
- queries: bfloat16 [2, 8192, 2560], P('dp', 'ctx', 'head'), may hold values from -25 to 25
- keys: bfloat16 [2, 8192, 2560], P('dp', 'ctx', 'head'), may hold values from -25 to 25
- values: bfloat16 [2, 8192, 2560], P('dp', 'ctx', 'head'), may hold values from -6 to 6
- grad_y: bfloat16 [2, 8192, 2560], P('dp', 'ctx', 'head'), may hold values from -6 to 6
- out_gain: float32 [2560], P('head'), may hold values from 0.1 to 1.9
- offsets: int32 [2, 20], P(None, 'head'), may hold values from 0 to 63, as said below
Outputs:
- attended: bfloat16 [2, 8192, 2560], P('dp', 'ctx', 'head')
- query_grad: bfloat16 [2, 8192, 2560], P('dp', 'ctx', 'head')
- key_grad: bfloat16 [2, 8192, 2560], P('dp', 'ctx', 'head')
- value_grad: bfloat16 [2, 8192, 2560], P('dp', 'ctx', 'head')
- gain_grad: float32 [2560], P('head')
Inputs may be any that keep to these rules, and one draw needn't show every extreme that they name: Row 0 holds offsets below 8, row 1 offsets below 64.
All inputs are finite; a program needn't handle non-finite values.
Results may differ from a plain program's by a relative error of at most 0.011.
Values may be sent and summed in bfloat16 or wider, within the bound.
A program may use at most 64 MiB of HBM per device.

v0:
```python
import math
import jax
import jax.numpy as jnp
from jax import lax
from jax.sharding import PartitionSpec as P

HEAD_DIM = 128
SPAN = 4
R1 = 8
EPS = 1e-06


def group_gather(block, axis, group):
    count = lax.axis_size(axis)
    pieces = [block]
    for shift in range(1, group):
        route = []
        for src in range(count):
            base = src - src % group
            route.append((src, base + (src % group + shift) % group))
        pieces.append(lax.ppermute(block, axis, route))
    return jnp.concatenate(pieces, 0)


def pick_rows(source_rows, dilation, shifts):
    row_count, head_count, head_width = source_rows.shape
    grouped = source_rows.reshape(row_count // dilation, dilation, head_count, head_width)
    hit_mask = jnp.arange(dilation, dtype=jnp.int32).reshape(1, dilation, 1, 1) == shifts.reshape(
        1, 1, head_count, 1
    )
    chosen = jnp.where(hit_mask, grouped, jnp.zeros((), source_rows.dtype))
    return jnp.sum(chosen, axis=1, dtype=source_rows.dtype)


def place_rows(row_values, dilation, shifts):
    row_count, head_count, head_width = row_values.shape
    hit_mask = jnp.arange(dilation, dtype=jnp.int32).reshape(1, dilation, 1, 1) == shifts.reshape(
        1, 1, head_count, 1
    )
    spread = jnp.where(hit_mask, row_values[:, None], jnp.zeros((), row_values.dtype))
    return spread.reshape(row_count * dilation, head_count, head_width)


def level_scores(q_rows, k_rows):
    score_scale = 1.0 / math.sqrt(q_rows.shape[-1])
    return (
        jnp.einsum("qhe,khe->hqk", q_rows, k_rows, preferred_element_type=jnp.float32) * score_scale
    )


def attend(q_rows, k_rows, v_rows):
    scores = level_scores(q_rows, k_rows)
    row_max = jnp.max(scores, axis=-1, keepdims=True)
    log_total = row_max[..., 0] + jnp.log(jnp.sum(jnp.exp(scores - row_max), axis=-1))
    soft_rows = jnp.exp(scores - log_total[..., None]).astype(jnp.bfloat16)
    level_out = jnp.einsum("hqk,khe->qhe", soft_rows, v_rows, preferred_element_type=jnp.float32)
    return (level_out, log_total.T)


def score_grads(q_rows, k_rows, v_rows, log_total, grad_low, row_shift):
    score_scale = 1.0 / math.sqrt(q_rows.shape[-1])
    scores = level_scores(q_rows, k_rows)
    exact_soft = jnp.exp(scores - log_total.T[..., None])
    prob_grad = jnp.einsum("qhe,khe->hqk", grad_low, v_rows, preferred_element_type=jnp.float32)
    score_grad = (exact_soft * (prob_grad + row_shift.T[..., None]) * score_scale).astype(
        jnp.bfloat16
    )
    return (score_grad, exact_soft.astype(jnp.bfloat16))


def key_parts(score_grad, soft_low, q_rows, grad_low):
    k_part = jnp.einsum("hqk,qhe->khe", score_grad, q_rows, preferred_element_type=jnp.float32)
    v_part = jnp.einsum("hqk,qhe->khe", soft_low, grad_low, preferred_element_type=jnp.float32)
    return (k_part, v_part)


def query_part(score_grad, k_rows):
    return jnp.einsum("hqk,khe->qhe", score_grad, k_rows, preferred_element_type=jnp.float32)


def split_qkv(packed, head_count):
    width = head_count * HEAD_DIM
    shape = (packed.shape[0], head_count, HEAD_DIM)
    return tuple((packed[:, i * width : (i + 1) * width].reshape(shape) for i in range(3)))


def pack_grads(grad_low, row_shift):
    rows = grad_low.shape[0]
    return jnp.concatenate(
        [grad_low.astype(jnp.float32).reshape(rows, -1), row_shift.astype(jnp.float32)], 1
    )


def unpack_grads(packed, head_count):
    width = head_count * HEAD_DIM
    grad_low = packed[:, :width].astype(jnp.bfloat16).reshape(-1, head_count, HEAD_DIM)
    return (grad_low, packed[:, width:])


def shards(queries, keys, values, grad_y, out_gain, offsets):
    tokens = queries.shape[1]
    flat_width = queries.shape[2]
    head_count = flat_width // HEAD_DIM
    row_shape = (tokens, head_count, HEAD_DIM)
    q_own = queries[0].reshape(row_shape)
    k_own = keys[0].reshape(row_shape)
    v_own = values[0].reshape(row_shape)
    ctx_size = lax.axis_size("ctx")
    my_place = lax.axis_index("ctx")
    mid_shift = offsets[0]
    top_shift = offsets[1]
    positions = jnp.arange(tokens, dtype=jnp.int32)
    mid_hit = (positions % R1)[:, None] == mid_shift[None, :]
    top_hit = (positions % ctx_size)[:, None] == top_shift[None, :]
    mid_pack = jnp.concatenate(
        [pick_rows(x, R1, mid_shift).reshape(-1, flat_width) for x in (q_own, k_own, v_own)], 1
    )
    top_pack = jnp.concatenate(
        [pick_rows(x, ctx_size, top_shift).reshape(-1, flat_width) for x in (q_own, k_own, v_own)],
        1,
    )
    mid_rows = mid_pack.shape[0]
    top_rows = top_pack.shape[0]
    mid_all = group_gather(mid_pack, "ctx", SPAN)
    top_all = lax.all_gather(top_pack, "ctx", axis=0, tiled=True)
    mid_q, mid_k, mid_v = split_qkv(mid_all, head_count)
    top_q, top_k, top_v = split_qkv(top_all, head_count)
    top_start = my_place * top_rows
    base_out, base_total = attend(q_own, k_own, v_own)
    mid_out_all, mid_total_all = attend(mid_q, mid_k, mid_v)
    top_out_all, top_total_all = attend(top_q, top_k, top_v)
    mid_out = mid_out_all[:mid_rows]
    mid_total = mid_total_all[:mid_rows]
    top_out = lax.dynamic_slice_in_dim(top_out_all, top_start, top_rows, 0)
    top_total = lax.dynamic_slice_in_dim(top_total_all, top_start, top_rows, 0)
    mid_full = place_rows(mid_total[..., None], R1, mid_shift)[..., 0]
    top_full = place_rows(top_total[..., None], ctx_size, top_shift)[..., 0]
    row_max = jnp.maximum(base_total, jnp.where(mid_hit, mid_full, base_total))
    row_max = jnp.maximum(row_max, jnp.where(top_hit, top_full, base_total))
    base_expo = jnp.exp(base_total - row_max)
    mid_expo = jnp.where(mid_hit, jnp.exp(mid_full - row_max), 0.0)
    top_expo = jnp.where(top_hit, jnp.exp(top_full - row_max), 0.0)
    denom = base_expo + mid_expo + top_expo
    base_share = base_expo / denom
    mid_share = mid_expo / denom
    top_share = top_expo / denom
    attn = (
        base_share[..., None] * base_out
        + mid_share[..., None] * place_rows(mid_out, R1, mid_shift)
        + top_share[..., None] * place_rows(top_out, ctx_size, top_shift)
    )
    inv_rms = lax.rsqrt(jnp.mean(attn * attn, axis=-1, keepdims=True) + EPS)
    normed = attn * inv_rms
    gain_rows = out_gain.reshape(head_count, HEAD_DIM)
    attended = (normed * gain_rows).astype(jnp.bfloat16).reshape(1, tokens, flat_width)
    grad_full = grad_y[0].reshape(row_shape).astype(jnp.float32)
    gain_part = jnp.sum(grad_full * normed, axis=0).reshape(flat_width)
    gain_grad = lax.psum(gain_part, ("dp", "ctx"))
    grad_norm = grad_full * gain_rows
    grad_attn = inv_rms * (
        grad_norm - normed * jnp.mean(grad_norm * normed, axis=-1, keepdims=True)
    )
    inner = jnp.sum(grad_attn * attn, axis=-1)
    base_low = (base_share[..., None] * grad_attn).astype(jnp.bfloat16)
    base_shift = -(base_share * inner)
    base_grad, base_soft = score_grads(q_own, k_own, v_own, base_total, base_low, base_shift)
    base_dq = query_part(base_grad, k_own)
    base_dk, base_dv = key_parts(base_grad, base_soft, q_own, base_low)
    mid_sel = pick_rows(mid_share[..., None], R1, mid_shift)[..., 0]
    mid_low = (mid_sel[..., None] * pick_rows(grad_attn, R1, mid_shift)).astype(jnp.bfloat16)
    mid_row_shift = -(mid_sel * pick_rows(inner[..., None], R1, mid_shift)[..., 0])
    top_sel = pick_rows(top_share[..., None], ctx_size, top_shift)[..., 0]
    top_low = (top_sel[..., None] * pick_rows(grad_attn, ctx_size, top_shift)).astype(jnp.bfloat16)
    top_row_shift = -(top_sel * pick_rows(inner[..., None], ctx_size, top_shift)[..., 0])
    mid_low_all, mid_shift_all = unpack_grads(
        group_gather(pack_grads(mid_low, mid_row_shift), "ctx", SPAN), head_count
    )
    top_low_all, top_shift_all = unpack_grads(
        lax.all_gather(pack_grads(top_low, top_row_shift), "ctx", axis=0, tiled=True), head_count
    )
    mid_grad, mid_soft = score_grads(mid_q, mid_k, mid_v, mid_total_all, mid_low_all, mid_shift_all)
    mid_dq = query_part(mid_grad[:, :mid_rows], mid_k)
    mid_dk, mid_dv = key_parts(
        mid_grad[:, :, :mid_rows], mid_soft[:, :, :mid_rows], mid_q, mid_low_all
    )
    top_grad, top_soft = score_grads(top_q, top_k, top_v, top_total_all, top_low_all, top_shift_all)
    own_grad = lax.dynamic_slice_in_dim(top_grad, top_start, top_rows, 1)
    top_dq = query_part(own_grad, top_k)
    key_grad_cols = lax.dynamic_slice_in_dim(top_grad, top_start, top_rows, 2)
    key_soft_cols = lax.dynamic_slice_in_dim(top_soft, top_start, top_rows, 2)
    top_dk, top_dv = key_parts(key_grad_cols, key_soft_cols, top_q, top_low_all)
    query_grad = (
        base_dq + place_rows(mid_dq, R1, mid_shift) + place_rows(top_dq, ctx_size, top_shift)
    )
    key_grad = base_dk + place_rows(mid_dk, R1, mid_shift) + place_rows(top_dk, ctx_size, top_shift)
    value_grad = (
        base_dv + place_rows(mid_dv, R1, mid_shift) + place_rows(top_dv, ctx_size, top_shift)
    )
    out_shape = (1, tokens, flat_width)
    return (
        attended,
        query_grad.astype(jnp.bfloat16).reshape(out_shape),
        key_grad.astype(jnp.bfloat16).reshape(out_shape),
        value_grad.astype(jnp.bfloat16).reshape(out_shape),
        gain_grad,
    )


def solution(mesh):
    in_specs = (
        P("dp", "ctx", "head"),
        P("dp", "ctx", "head"),
        P("dp", "ctx", "head"),
        P("dp", "ctx", "head"),
        P("head"),
        P(None, "head"),
    )
    out_specs = (
        P("dp", "ctx", "head"),
        P("dp", "ctx", "head"),
        P("dp", "ctx", "head"),
        P("dp", "ctx", "head"),
        P("head"),
    )
    return jax.shard_map(shards, mesh=mesh, in_specs=in_specs, out_specs=out_specs, check_vma=False)
```

profile of v0, /device:TPU:256, one launch (start us, length us, event | category | flops | bytes accessed | tf_op | source)
XLA Modules:
  0.0 428.5 jit_solution(14037007713612233846)
XLA Ops:
  0.6 0.8 slice_bitcast_fusion.5
  1.4 0.6 copy-done.23
  2.0 1.5 fusion.24
  3.6 5.5 %collective-permute-start.2 = (bf16[16,1920]{1,0:T(8,128)(2,1)S(1)}, bf16[16,1920]{1,0:T(8,128)(2,1)S(1)}, u32[]{:S(2)}, u32[]{:S(2)}) collective-permute-start(bf16[16,1920]{1,0:T(8,128)(2,1)S(1)} %bitcast_dynamic-update-slice_fusion), channel_id=1, source_target_pairs={{0,12},{4,0},{8,4},{12,8},{16,28},{20,16},{24,20},{28,24},{32,44},... | collective-permute-start | bytes 184328 | tf_op jit(solution)/shard_map/ppermute | solution.py:21
  9.1 1.9 collective-permute-start.1
  11.0 2.9 collective-permute-start
  14.1 0.7 copy-done.1
  15.1 0.7 copy-done.2
  16.0 0.2 reshape_reshape_squeeze.21
  16.2 0.2 reshape_reshape_squeeze.22
  16.4 0.2 reshape_reshape_squeeze.23
  16.8 0.4 copy-done.21
  17.2 0.7 broadcast_in_dim.285
  17.9 0.6 broadcast_in_dim.278
  18.9 0.3 select_reduce_fusion.2
  19.2 50.0 %all-gather = bf16[64,2,1920]{2,1,0:T(2,128)(2,1)S(1)} all-gather(bf16[1,2,1920]{2,1,0:T(2,128)(2,1)S(1)} %maximum_bitcast_fusion.1), channel_id=1, replica_groups=mesh['dp'=2,'ctx'=64,'head'=4] {'ctx'}, dimensions={0}, use_global_device_ids=true | all-gather | bytes 499200 | tf_op jit(solution)/shard_map/all_gather | solution.py:125
  69.2 0.2 reshape.370
  69.9 0.3 fusion.67
  70.4 0.5 copy-done.7
  71.0 0.7 broadcast_in_dim.289
  71.7 0.3 fusion.70
  72.0 0.3 fusion.69
  72.5 0.2 fusion.68
  72.8 0.5 copy-done.9
  73.5 0.2 convolution_bitcast_fusion.4
  73.8 0.4 copy-done.19
  74.1 0.3 copy-done.18
  74.7 0.2 fusion.20
  74.9 0.5 multiply_reduce_fusion.3
  75.5 0.7 copy-done.13
  76.1 0.8 multiply_reduce_fusion
  76.9 0.7 copy-done.15
  77.6 0.3 fusion.19
  78.0 0.6 negate_bitcast_fusion
  79.1 0.6 pad_maximum_fusion.2
  79.7 2.6 collective-permute-start.5
  82.3 3.1 collective-permute-start.4
  85.4 2.3 collective-permute-start.3
  87.7 0.2 fusion.18
  88.0 0.4 copy-done.22
  88.7 49.2 %all-gather.1 = f32[64,2,645]{2,1,0:T(2,128)S(1)} all-gather(f32[1,2,645]{2,1,0:T(2,128)S(1)} %maximum_bitcast_fusion.2), channel_id=1, replica_groups=mesh['dp'=2,'ctx'=64,'head'=4] {'ctx'}, dimensions={0}, use_global_device_ids=true | all-gather | bytes 335400 | tf_op jit(solution)/shard_map/all_gather | solution.py:179
  137.9 0.3 reshape.372
  138.2 0.7 slice.99
  138.9 0.4 fusion.17
  139.3 0.5 copy-done.3
  140.0 0.2 convolution_bitcast_fusion.9
  140.1 0.5 copy-done.8
  140.7 0.3 fusion.16
  141.1 0.4 convolution_bitcast_fusion.8
  141.5 0.2 copy.319
  141.7 0.8 copy.357
  142.7 0.5 copy-done.17
  143.2 277.9 %psum.7 = f32[640]{0:T(1024)} all-reduce(f32[640]{0:T(1024)S(1)} %bitcast.273), channel_id=1, replica_groups=mesh['dp'=2,'ctx'=64,'head'=4] {'dp','ctx'}, use_global_device_ids=true, to_apply=%region_22.23 | all-reduce | flops 640 | bytes 5120 | tf_op jit(solution)/shard_map/psum | solution.py:158
  421.1 0.9 pad_maximum_fusion.1
  422.1 0.8 maximum_bitcast_fusion
  423.0 0.5 copy-done.10
  423.9 0.2 convolution_bitcast_fusion.7
  424.1 0.6 copy-done.12
  424.7 0.2 fusion.14
  425.1 0.8 copy.359
  426.0 0.3 fusion.13
  426.4 0.8 copy.358
  427.2 0.3 fusion.15
  427.7 0.8 copy.360
  (112 shorter events, 5.3 us)
Async XLA Ops:
  1.4 0.6 copy-start.23
  1.4 15.2 %copy-start.25 = (s32[5]{0:T(128)}, s32[5]{0:T(128)S(1)}, u32[]{:S(2)}) copy-start(s32[5]{0:T(128)S(1)} %get-tuple-element.62) | copy-start | bytes 64
  2.0 15.9 %copy-start.14 = (pred[8,5]{0,1:T(8,128)(4,1)}, pred[8,5]{0,1:T(8,128)(4,1)S(1)}, u32[]{:S(2)}) copy-start(pred[8,5]{0,1:T(8,128)(4,1)S(1)} %iota_compare_fusion.1) | copy-start | bytes 124
  2.0 11.9 %copy-start = (bf16[1,128,640]{2,1,0:T(8,128)(2,1)S(1)}, bf16[1,128,640]{2,1,0:T(8,128)(2,1)}, u32[]{:S(2)}) copy-start(bf16[1,128,640]{2,1,0:T(8,128)(2,1)} %param.6) | copy-start | bytes 491524
  3.6 68.8 %collective-permute-start.2 = (bf16[16,1920]{1,0:T(8,128)(2,1)S(1)}, bf16[16,1920]{1,0:T(8,128)(2,1)S(1)}, u32[]{:S(2)}, u32[]{:S(2)}) collective-permute-start(bf16[16,1920]{1,0:T(8,128)(2,1)S(1)} %bitcast_dynamic-update-slice_fusion), channel_id=1, source_target_pairs={{0,12},{4,0},{8,4},{12,8},{16,28},{20,16},{24,20},{28,24},{32,44},... | collective-permute-start | bytes 184328 | tf_op jit(solution)/shard_map/ppermute | solution.py:21
  9.1 63.3 %collective-permute-start.1 = (bf16[16,1920]{1,0:T(8,128)(2,1)S(1)}, bf16[16,1920]{1,0:T(8,128)(2,1)S(1)}, u32[]{:S(2)}, u32[]{:S(2)}) collective-permute-start(bf16[16,1920]{1,0:T(8,128)(2,1)S(1)} %bitcast_dynamic-update-slice_fusion), channel_id=1, source_target_pairs={{0,8},{4,12},{8,0},{12,4},{16,24},{20,28},{24,16},{28,20},{32,40},... | collective-permute-start | bytes 184328 | tf_op jit(solution)/shard_map/ppermute | solution.py:21
  11.0 61.3 %collective-permute-start = (bf16[16,1920]{1,0:T(8,128)(2,1)S(1)}, bf16[16,1920]{1,0:T(8,128)(2,1)S(1)}, u32[]{:S(2)}, u32[]{:S(2)}) collective-permute-start(bf16[16,1920]{1,0:T(8,128)(2,1)S(1)} %bitcast_dynamic-update-slice_fusion), channel_id=1, source_target_pairs={{0,4},{4,8},{8,12},{12,0},{16,20},{20,24},{24,28},{28,16},{32,36},... | collective-permute-start | bytes 184328 | tf_op jit(solution)/shard_map/ppermute | solution.py:21
  14.0 0.9 copy-start.1
  14.9 0.9 copy-start.2
  16.4 2.2 copy-start.6
  16.7 0.5 copy-start.21
  70.3 0.6 copy-start.7
  72.4 1.0 copy-start.4
  72.7 0.6 copy-start.9
  73.5 0.7 copy-start.19
  73.5 0.7 copy-start.26
  73.7 0.7 copy-start.18
  73.7 0.7 copy-start.11
  73.8 0.7 copy-start.24
  75.4 0.7 copy-start.13
  76.9 0.7 copy-start.15
  79.7 341.3 %collective-permute-start.5 = (f32[16,645]{1,0:T(8,128)}, f32[16,645]{1,0:T(8,128)}, u32[]{:S(2)}, u32[]{:S(2)}) collective-permute-start(f32[16,645]{1,0:T(8,128)} %pad_maximum_fusion.2), channel_id=1, source_target_pairs={{0,12},{4,0},{8,4},{12,8},{16,28},{20,16},{24,20},{28,24},{32,44},... | collective-permute-start | bytes 123848 | tf_op jit(solution)/shard_map/ppermute | solution.py:21
  82.3 338.8 %collective-permute-start.4 = (f32[16,645]{1,0:T(8,128)}, f32[16,645]{1,0:T(8,128)}, u32[]{:S(2)}, u32[]{:S(2)}) collective-permute-start(f32[16,645]{1,0:T(8,128)} %pad_maximum_fusion.2), channel_id=1, source_target_pairs={{0,8},{4,12},{8,0},{12,4},{16,24},{20,28},{24,16},{28,20},{32,40},... | collective-permute-start | bytes 123848 | tf_op jit(solution)/shard_map/ppermute | solution.py:21
  85.4 335.7 %collective-permute-start.3 = (f32[16,645]{1,0:T(8,128)}, f32[16,645]{1,0:T(8,128)}, u32[]{:S(2)}, u32[]{:S(2)}) collective-permute-start(f32[16,645]{1,0:T(8,128)} %pad_maximum_fusion.2), channel_id=1, source_target_pairs={{0,4},{4,8},{8,12},{12,0},{16,20},{20,24},{24,28},{28,16},{32,36},... | collective-permute-start | bytes 123848 | tf_op jit(solution)/shard_map/ppermute | solution.py:21
  87.7 0.6 copy-start.22
  138.2 0.7 copy-start.16
  138.9 0.9 copy-start.3
  140.0 0.7 copy-start.8
  141.7 0.8 copy-start.20
  142.5 0.7 copy-start.17
  422.1 0.9 copy-start.5
  422.8 0.7 copy-start.10
  424.1 0.6 copy-start.12
where the time goes:
time: 429 us
  blocking collectives  377 us (88%)
  local copies, waits for them, and re-layouts  19.9 us (5%)
  starting transfers between devices  18.3 us (4%)
  other arithmetic  7.42 us (2%)
  matrix products  4.56 us (1%)
    psum x1, blocking collectives, shards(): gain_grad = lax.psum(gain_part, ('dp', 'ctx'))  278 us
    all_gather x1, blocking collectives, shards(): top_all = lax.all_gather(top_pack, 'ctx', axis=0, tiled=True)  50 us
    all_gather x1, blocking collectives, shards(): lax.all_gather(pack_grads(top_low, top_row_shift), 'ctx', axis=0, tiled=T...  49.2 us
    ppermute x6, starting transfers between devices, group_gather(): pieces.append(lax.ppermute(block, axis, route))  18.3 us
    unnamed x69, local copies, waits for them, and re-layouts  13.1 us
  transfers between devices with their start and end apart: 6, of which 0 were waited for; matrix products, arithmetic and copies ran while one was open for 2% of the time, Pallas kernels for 0%

commit v1 on v0

--- a/solution.py
+++ b/solution.py
@@ -176,7 +176,13 @@
         group_gather(pack_grads(mid_low, mid_row_shift), "ctx", SPAN), head_count
     )
     top_low_all, top_shift_all = unpack_grads(
-        lax.all_gather(pack_grads(top_low, top_row_shift), "ctx", axis=0, tiled=True), head_count
+        jnp.concatenate(
+            lax.all_to_all(
+                jnp.stack([pack_grads(top_low, top_row_shift)] * lax.axis_size("ctx")), "ctx", 0, 0
+            ),
+            axis=0,
+        ),
+        head_count,
     )
     mid_grad, mid_soft = score_grads(mid_q, mid_k, mid_v, mid_total_all, mid_low_all, mid_shift_all)
     mid_dq = query_part(mid_grad[:, :mid_rows], mid_k)

time: 429 us -> 386 us (0.90)
  the two profiles are of different devices: /device:TPU:256 before, /device:TPU:258 now
where the time goes in v1:
time: 386 us; the launch traced here: 385 us
  blocking collectives  328 us (85%)
  starting transfers between devices  30.3 us (8%)
  local copies, waits for them, and re-layouts  15.9 us (4%)
  other arithmetic  5.21 us (1%)
  matrix products  4.57 us (1%)
    psum x1, blocking collectives, shards(): gain_grad = lax.psum(gain_part, ('dp', 'ctx'))  278 us
    all_gather x1, blocking collectives, shards(): top_all = lax.all_gather(top_pack, 'ctx', axis=0, tiled=True)  50 us
    ppermute x6, starting transfers between devices, group_gather(): pieces.append(lax.ppermute(block, axis, route))  18.3 us
    all_to_all x1, starting transfers between devices, shards(): lax.all_to_all(jnp.stack([pack_grads(top_low, top_row_shift)] * lax.axis_...  12 us
    unnamed x54, local copies, waits for them, and re-layouts  10.3 us
  transfers between devices with their start and end apart: 7, of which 0 were waited for; matrix products, arithmetic and copies ran while one was open for 2% of the time, Pallas kernels for 0%

profile of v1, /device:TPU:258, one launch (start us, length us, event | category | flops | bytes accessed | tf_op | source)
XLA Modules:
  0.0 385.3 jit_solution(10244286904732172255)
XLA Ops:
  0.6 0.8 slice_bitcast_fusion.5
  1.5 1.5 fusion.24
  3.0 5.5 %collective-permute-start.2 = (bf16[16,1920]{1,0:T(8,128)(2,1)S(1)}, bf16[16,1920]{1,0:T(8,128)(2,1)S(1)}, u32[]{:S(2)}, u32[]{:S(2)}) collective-permute-start(bf16[16,1920]{1,0:T(8,128)(2,1)S(1)} %bitcast_dynamic-update-slice_fusion), channel_id=1, source_target_pairs={{0,12},{4,0},{8,4},{12,8},{16,28},{20,16},{24,20},{28,24},{32,44},... | collective-permute-start | bytes 184328 | tf_op jit(solution)/shard_map/ppermute | solution.py:21
  8.5 1.9 collective-permute-start.1
  10.5 2.9 collective-permute-start
  13.4 0.2 copy.294
  13.6 0.7 copy-done.1
  14.5 0.7 copy-done.2
  15.4 0.2 reshape_reshape_squeeze.21
  15.6 0.2 reshape_reshape_squeeze.22
  15.8 0.2 reshape_reshape_squeeze.23
  16.2 0.4 copy-done.18
  17.2 0.3 select_reduce_fusion.2
  17.5 50.0 %all-gather = bf16[64,2,1920]{2,1,0:T(2,128)(2,1)S(1)} all-gather(bf16[1,2,1920]{2,1,0:T(2,128)(2,1)S(1)} %maximum_bitcast_fusion.1), channel_id=1, replica_groups=mesh['dp'=2,'ctx'=64,'head'=4] {'ctx'}, dimensions={0}, use_global_device_ids=true | all-gather | bytes 499200 | tf_op jit(solution)/shard_map/all_gather | solution.py:125
  67.5 0.2 reshape.376
  67.9 0.2 copy.316
  68.1 0.2 copy.307
  68.3 0.3 fusion.67
  68.7 0.5 copy-done.8
  69.5 0.3 fusion.70
  69.8 0.3 fusion.69
  70.2 0.2 fusion.68
  70.5 0.5 copy-done.10
  71.2 0.2 convolution_bitcast_fusion.4
  71.7 0.2 fusion.20
  72.0 0.5 multiply_reduce_fusion.3
  72.5 0.7 copy-done.14
  73.2 0.8 multiply_reduce_fusion
  74.0 0.3 fusion.19
  74.2 0.2 multiply_reduce_fusion.1
  74.9 0.6 pad_maximum_fusion.2
  75.5 2.6 collective-permute-start.5
  78.1 3.1 collective-permute-start.4
  81.2 2.3 collective-permute-start.3
  83.5 0.2 fusion.18
  83.8 0.4 fusion.17
  84.2 0.3 copy-done.19
  84.8 0.2 copy.319
  85.0 0.8 copy.357
  85.8 0.8 stack.2
  86.7 12.0 %all-to-all-start = ((f32[64,2,645]{2,1,0:T(2,128)}), f32[64,2,645]{2,1,0:T(2,128)S(1)}, u32[]{:S(2)}, u32[]{:S(2)}) async-start(f32[64,2,645]{2,1,0:T(2,128)} %stack.2), calls=%async_computation | async-start | bytes 786432 | tf_op jit(solution)/shard_map/all_to_all | solution.py:180
  98.7 278.1 %psum.7 = f32[640]{0:T(1024)} all-reduce(f32[640]{0:T(1024)S(1)} %bitcast.271), channel_id=1, replica_groups=mesh['dp'=2,'ctx'=64,'head'=4] {'dp','ctx'}, use_global_device_ids=true, to_apply=%region_22.23 | all-reduce | flops 640 | bytes 5120 | tf_op jit(solution)/shard_map/psum | solution.py:158
  376.9 0.7 copy-done.11
  377.6 0.2 multiply_convert_fusion.2
  378.0 0.2 convolution_bitcast_fusion.7
  378.2 0.3 reshape.366
  378.6 0.2 copy.337
  378.8 0.2 convolution_bitcast_fusion.9
  379.0 0.5 copy-done.9
  379.5 0.3 fusion.16
  379.8 0.2 convolution_bitcast_fusion.10
  380.0 0.4 convolution_bitcast_fusion.8
  380.3 0.3 copy-done.17
  380.7 0.2 bitcast_select_fusion
  380.9 0.7 copy-done.13
  381.5 0.2 fusion.14
  381.8 0.2 copy.349
  381.9 0.8 copy.359
  382.8 0.3 fusion.13
  383.0 0.2 copy.344
  383.2 0.8 copy.358
  384.0 0.3 fusion.15
  384.3 0.2 copy.355
  384.5 0.8 copy.360
  (100 shorter events, 3.7 us)
Async XLA Ops:
  1.5 11.9 %copy-start = (bf16[1,128,640]{2,1,0:T(8,128)(2,1)S(1)}, bf16[1,128,640]{2,1,0:T(8,128)(2,1)}, u32[]{:S(2)}) copy-start(bf16[1,128,640]{2,1,0:T(8,128)(2,1)} %param.6) | copy-start | bytes 491524
  3.0 67.1 %collective-permute-start.2 = (bf16[16,1920]{1,0:T(8,128)(2,1)S(1)}, bf16[16,1920]{1,0:T(8,128)(2,1)S(1)}, u32[]{:S(2)}, u32[]{:S(2)}) collective-permute-start(bf16[16,1920]{1,0:T(8,128)(2,1)S(1)} %bitcast_dynamic-update-slice_fusion), channel_id=1, source_target_pairs={{0,12},{4,0},{8,4},{12,8},{16,28},{20,16},{24,20},{28,24},{32,44},... | collective-permute-start | bytes 184328 | tf_op jit(solution)/shard_map/ppermute | solution.py:21
  8.5 61.6 %collective-permute-start.1 = (bf16[16,1920]{1,0:T(8,128)(2,1)S(1)}, bf16[16,1920]{1,0:T(8,128)(2,1)S(1)}, u32[]{:S(2)}, u32[]{:S(2)}) collective-permute-start(bf16[16,1920]{1,0:T(8,128)(2,1)S(1)} %bitcast_dynamic-update-slice_fusion), channel_id=1, source_target_pairs={{0,8},{4,12},{8,0},{12,4},{16,24},{20,28},{24,16},{28,20},{32,40},... | collective-permute-start | bytes 184328 | tf_op jit(solution)/shard_map/ppermute | solution.py:21
  10.5 59.7 %collective-permute-start = (bf16[16,1920]{1,0:T(8,128)(2,1)S(1)}, bf16[16,1920]{1,0:T(8,128)(2,1)S(1)}, u32[]{:S(2)}, u32[]{:S(2)}) collective-permute-start(bf16[16,1920]{1,0:T(8,128)(2,1)S(1)} %bitcast_dynamic-update-slice_fusion), channel_id=1, source_target_pairs={{0,4},{4,8},{8,12},{12,0},{16,20},{20,24},{24,28},{28,16},{32,36},... | collective-permute-start | bytes 184328 | tf_op jit(solution)/shard_map/ppermute | solution.py:21
  13.4 0.9 copy-start.1
  14.3 0.9 copy-start.2
  15.8 1.1 copy-start.3
  16.1 0.6 copy-start.18
  16.8 55.0 %copy-start.16 = (pred[128,5]{0,1:T(8,128)(4,1)}, pred[128,5]{0,1:T(8,128)(4,1)S(1)}, u32[]{:S(2)}) copy-start(pred[128,5]{0,1:T(8,128)(4,1)S(1)} %broadcast_in_dim.285) | copy-start | bytes 1924
  16.9 55.1 %copy-start.12 = (pred[128,5]{0,1:T(8,128)(4,1)}, pred[128,5]{0,1:T(8,128)(4,1)S(1)}, u32[]{:S(2)}) copy-start(pred[128,5]{0,1:T(8,128)(4,1)S(1)} %broadcast_in_dim.278) | copy-start | bytes 1924
  68.6 0.6 copy-start.8
  70.4 0.6 copy-start.10
  71.5 12.2 %copy-start.4 = (f32[128,5]{0,1:T(8,128)}, f32[128,5]{0,1:T(8,128)S(1)}, u32[]{:S(2)}) copy-start(f32[128,5]{0,1:T(8,128)S(1)} %get-tuple-element.44) | copy-start | bytes 7684
  71.5 12.2 %copy-start.6 = (f32[5,128]{1,0:T(8,128)}, f32[5,128]{1,0:T(8,128)S(1)}, u32[]{:S(2)}) copy-start(f32[5,128]{1,0:T(8,128)S(1)} %get-tuple-element.48) | copy-start | bytes 7684
  72.5 0.7 copy-start.14
  75.5 301.3 %collective-permute-start.5 = (f32[16,645]{1,0:T(8,128)}, f32[16,645]{1,0:T(8,128)S(1)}, u32[]{:S(2)}, u32[]{:S(2)}) collective-permute-start(f32[16,645]{1,0:T(8,128)} %pad_maximum_fusion.2), channel_id=1, source_target_pairs={{0,12},{4,0},{8,4},{12,8},{16,28},{20,16},{24,20},{28,24},{32,44},... | collective-permute-start | bytes 123848 | tf_op jit(solution)/shard_map/ppermute | solution.py:21
  78.1 298.7 %collective-permute-start.4 = (f32[16,645]{1,0:T(8,128)}, f32[16,645]{1,0:T(8,128)S(1)}, u32[]{:S(2)}, u32[]{:S(2)}) collective-permute-start(f32[16,645]{1,0:T(8,128)} %pad_maximum_fusion.2), channel_id=1, source_target_pairs={{0,8},{4,12},{8,0},{12,4},{16,24},{20,28},{24,16},{28,20},{32,40},... | collective-permute-start | bytes 123848 | tf_op jit(solution)/shard_map/ppermute | solution.py:21
  81.2 295.6 %collective-permute-start.3 = (f32[16,645]{1,0:T(8,128)}, f32[16,645]{1,0:T(8,128)S(1)}, u32[]{:S(2)}, u32[]{:S(2)}) collective-permute-start(f32[16,645]{1,0:T(8,128)} %pad_maximum_fusion.2), channel_id=1, source_target_pairs={{0,4},{4,8},{8,12},{12,0},{16,20},{20,24},{24,28},{28,16},{32,36},... | collective-permute-start | bytes 123848 | tf_op jit(solution)/shard_map/ppermute | solution.py:21
  83.8 0.7 copy-start.19
  86.7 12.0 %copy-start.15 = (f32[5,128]{1,0:T(8,128)S(1)}, f32[5,128]{1,0:T(8,128)}, u32[]{:S(2)}) copy-start(f32[5,128]{1,0:T(8,128)} %get-tuple-element.30) | copy-start | bytes 7684
  86.7 291.5 %all-to-all-start = ((f32[64,2,645]{2,1,0:T(2,128)}), f32[64,2,645]{2,1,0:T(2,128)S(1)}, u32[]{:S(2)}, u32[]{:S(2)}) async-start(f32[64,2,645]{2,1,0:T(2,128)} %stack.2), calls=%async_computation | async-start | bytes 786432 | tf_op jit(solution)/shard_map/all_to_all | solution.py:180
  376.9 0.7 copy-start.11
  378.8 0.7 copy-start.9
  380.0 0.7 copy-start.17
  380.8 0.7 copy-start.13
  383.2 0.8 copy-start.5
  383.2 0.8 copy-start.7
